TPU v7x, 128 devices: a whole 4x4x4 slice. The times are simulated.
128 devices in a mesh: space: 16 (over x_lo, y, core), tm: 8 (over x_hi, z).
Axes of the slice: x: 4 (x_hi: 2, x_lo: 2; x = x_hi * 2 + x_lo), y: 4, z: 4, core: 2. Of those that a mesh axis runs over, the one named last changes fastest.
Arguments:
- vectors: bfloat16 [8, 2, 3, 96, 8192], P('tm', None, None, None, 'space'), may hold values from -6 to 6
- momenta: int32 [2, 3], replicated, may hold values from -3 to 3
- offsets: int32 [16, 3], replicated, may hold values from 0 to 56, as said below
Outputs:
- elementals: float32 [8, 96, 2, 18432], P(None, 'space')
Inputs may be any that keep to these rules, and one draw needn't show every extreme that they name: `offsets`: each row is the corner of one block of 8 x 8 x 8 sites of the 64^3 lattice: its first two coordinates are multiples of 8, its third a multiple of 8; no two rows name the same block, so the blocks never intersect.
All inputs are finite; a program needn't handle non-finite values.
Results may differ from a plain program's by a relative error of at most 0.0055.
Values may be sent and summed in bfloat16 or wider, within the bound.
No kernel may reach another device: no remote copies, remote signals or barrier semaphores. Data moves between devices by JAX's collectives and lax.ppermute only.
A program may use at most 128 MiB of HBM per device.

v0:
```python
import math
import jax
import jax.numpy as jnp
from jax import lax
from jax.sharding import PartitionSpec as P

LAT = 64
BRICK = 8
BRICK_Z = 8


def local_coords(site):
    return jnp.stack([site // (BRICK * BRICK_Z), site // BRICK_Z % BRICK, site % BRICK_Z])


def phases(momenta, coords):
    product = jnp.sum(momenta[:, :, None] * coords[None, :, :], axis=1)
    angle = (product % LAT).astype(jnp.float32) * (2.0 * math.pi / LAT)
    return jnp.stack([jnp.cos(angle), jnp.sin(angle)], axis=1)


def complex_term(w_real, w_imag, v_real, v_imag):
    return (w_real * v_real - w_imag * v_imag, w_real * v_imag + w_imag * v_real)


def cross_rows(phase, row_vecs, vecs):
    rows_f = row_vecs.astype(jnp.float32)
    cosine = phase[:, 0][:, None, None, :]
    sine = phase[:, 1][:, None, None, :]
    real_w = cosine * rows_f[0][None] - sine * rows_f[1][None]
    imag_w = cosine * rows_f[1][None] + sine * rows_f[0][None]
    real_w = jnp.transpose(real_w, (2, 0, 1, 3))
    imag_w = jnp.transpose(imag_w, (2, 0, 1, 3))
    real_v = vecs[0].astype(jnp.float32)
    imag_v = vecs[1].astype(jnp.float32)
    real_parts = []
    imag_parts = []
    for colour in range(3):
        first = (colour + 1) % 3
        second = (colour + 2) % 3
        plus_re, plus_im = complex_term(
            real_w[:, :, first, None, :],
            imag_w[:, :, first, None, :],
            real_v[second][None, None],
            imag_v[second][None, None],
        )
        minus_re, minus_im = complex_term(
            real_w[:, :, second, None, :],
            imag_w[:, :, second, None, :],
            real_v[first][None, None],
            imag_v[first][None, None],
        )
        real_parts.append(plus_re - minus_re)
        imag_parts.append(plus_im - minus_im)
    stacked = jnp.stack([jnp.stack(real_parts, axis=3), jnp.stack(imag_parts, axis=3)], axis=3)
    return stacked.astype(jnp.bfloat16)


def mixing(vecs):
    real_v = vecs[0]
    imag_v = vecs[1]
    return jnp.stack([jnp.stack([real_v, imag_v], axis=1), jnp.stack([-imag_v, real_v], axis=1)])


def body(vectors, momenta, offsets):
    local = vectors[0]
    nvec = local.shape[2]
    sites = local.shape[3]
    groups = lax.axis_size("space")
    rows = nvec // groups
    width = 2 * nvec * nvec
    moments = momenta.shape[0]
    mine = lax.axis_index("space") * rows
    empty = jnp.zeros((rows, moments, width), jnp.float32)
    vec_piece = lax.all_gather(local.reshape(6 * nvec, sites), "space", axis=1, tiled=True)
    length = vec_piece.shape[1]
    block = math.gcd(length, sites)

    def advance(index, acc):
        vec_block = lax.dynamic_slice_in_dim(vec_piece, index * block, block, 1).reshape(
            2, 3, nvec, block
        )
        site_ids = index * block + jnp.arange(block, dtype=jnp.int32)
        brick_ids = site_ids // sites
        coords = local_coords(site_ids % sites) + jnp.transpose(
            jnp.take(offsets, brick_ids, axis=0)
        )
        phase_block = phases(momenta, coords)
        row_vecs = lax.dynamic_slice_in_dim(vec_block, mine, rows, 2)
        crossed = cross_rows(phase_block, row_vecs, vec_block)
        part = jnp.einsum(
            "imjqcg,qcrkg->imjrk", crossed, mixing(vec_block), preferred_element_type=jnp.float32
        )
        return acc + part.reshape(rows, moments, width)

    summed = lax.fori_loop(0, length // block, advance, empty)
    finished = summed * (1.0 / math.sqrt(sites * groups))
    gathered = lax.all_gather(finished[None], "tm", axis=0, tiled=True)
    return gathered


def solution(mesh):
    return jax.shard_map(
        body,
        mesh=mesh,
        in_specs=(P("tm", None, None, None, "space"), P(), P()),
        out_specs=P(None, "space", None, None),
        check_vma=False,
    )
```

profile of v0, /device:TPU:1, one launch (start us, length us, event | category | flops | bytes accessed | tf_op | source)
XLA Modules:
  0.0 420.6 jit_solution(780666687985766581)
XLA Ops:
  8.8 60.9 %all-gather.4.cloned.1.call-done = bf16[576,8192]{1,0:T(8,128)(2,1)} async-done(((bf16[576,512]{1,0:T(8,128)(2,1)}), bf16[576,8192]{1,0:T(8,128)(2,1)}) %all-gather.4.cloned.1.call-update) | async-done | bytes 9437200 | tf_op jit(solution)/shard_map/all_gather | solution.py:75
  69.7 240.3 %while.17 = (s32[]{:T(128)}, f32[6,2,18432]{2,1,0:T(2,128)S(1)}, s32[2,3]{0,1:T(4,128)S(1)}, s32[16,3]{1,0:T(8,128)S(1)}, bf16[576,8192]{1,0:T(8,128)(2,1)}, /*i...) while((s32[]{:T(128)}, f32[6,2,18432]{2,1,0:T(2,128)S(1)}, ...), condition=%wide.region_2.3_spmd.clone, body=%wide.region_0.2_spmd.clone.sunk | while | flops 1412249600 | bytes 46142696 | solution.py:96
  73.8 4.4 %subtract_convert_fusion.7 = (bf16[6,2,96,1,512]{4,2,3,1,0:T(8,128)(2,1)S(1)}, bf16[6,2,96,1,512]{4,2,3,1,0:T(8,128)(2,1)S(1)}, bf16[6,2,96,1,512]{4,2,3,1,0:T(8...) fusion(f32[96,512]{1,0:T(8,128)S(1)} %get-tuple-element.381, ...), kind=kLoop, calls=%fused_computation.12.clone.1 | loop fusion | flops 28311552 | bytes 8404992 | tf_op jit(solution)/shard_map/convert.7
  88.8 4.4 %subtract_convert_fusion.7 = (bf16[6,2,96,1,512]{4,2,3,1,0:T(8,128)(2,1)S(1)}, bf16[6,2,96,1,512]{4,2,3,1,0:T(8,128)(2,1)S(1)}, bf16[6,2,96,1,512]{4,2,3,1,0:T(8...) fusion(f32[96,512]{1,0:T(8,128)S(1)} %get-tuple-element.381, ...), kind=kLoop, calls=%fused_computation.12.clone.1 | loop fusion | flops 28311552 | bytes 8404992 | tf_op jit(solution)/shard_map/convert.7
  103.8 4.4 %subtract_convert_fusion.7 = (bf16[6,2,96,1,512]{4,2,3,1,0:T(8,128)(2,1)S(1)}, bf16[6,2,96,1,512]{4,2,3,1,0:T(8,128)(2,1)S(1)}, bf16[6,2,96,1,512]{4,2,3,1,0:T(8...) fusion(f32[96,512]{1,0:T(8,128)S(1)} %get-tuple-element.381, ...), kind=kLoop, calls=%fused_computation.12.clone.1 | loop fusion | flops 28311552 | bytes 8404992 | tf_op jit(solution)/shard_map/convert.7
  109.3 2.0 fusion.24
  118.9 4.4 %subtract_convert_fusion.7 = (bf16[6,2,96,1,512]{4,2,3,1,0:T(8,128)(2,1)S(1)}, bf16[6,2,96,1,512]{4,2,3,1,0:T(8,128)(2,1)S(1)}, bf16[6,2,96,1,512]{4,2,3,1,0:T(8...) fusion(f32[96,512]{1,0:T(8,128)S(1)} %get-tuple-element.381, ...), kind=kLoop, calls=%fused_computation.12.clone.1 | loop fusion | flops 28311552 | bytes 8404992 | tf_op jit(solution)/shard_map/convert.7
  133.9 4.4 %subtract_convert_fusion.7 = (bf16[6,2,96,1,512]{4,2,3,1,0:T(8,128)(2,1)S(1)}, bf16[6,2,96,1,512]{4,2,3,1,0:T(8,128)(2,1)S(1)}, bf16[6,2,96,1,512]{4,2,3,1,0:T(8...) fusion(f32[96,512]{1,0:T(8,128)S(1)} %get-tuple-element.381, ...), kind=kLoop, calls=%fused_computation.12.clone.1 | loop fusion | flops 28311552 | bytes 8404992 | tf_op jit(solution)/shard_map/convert.7
  148.9 4.4 %subtract_convert_fusion.7 = (bf16[6,2,96,1,512]{4,2,3,1,0:T(8,128)(2,1)S(1)}, bf16[6,2,96,1,512]{4,2,3,1,0:T(8,128)(2,1)S(1)}, bf16[6,2,96,1,512]{4,2,3,1,0:T(8...) fusion(f32[96,512]{1,0:T(8,128)S(1)} %get-tuple-element.381, ...), kind=kLoop, calls=%fused_computation.12.clone.1 | loop fusion | flops 28311552 | bytes 8404992 | tf_op jit(solution)/shard_map/convert.7
  163.9 4.4 %subtract_convert_fusion.7 = (bf16[6,2,96,1,512]{4,2,3,1,0:T(8,128)(2,1)S(1)}, bf16[6,2,96,1,512]{4,2,3,1,0:T(8,128)(2,1)S(1)}, bf16[6,2,96,1,512]{4,2,3,1,0:T(8...) fusion(f32[96,512]{1,0:T(8,128)S(1)} %get-tuple-element.381, ...), kind=kLoop, calls=%fused_computation.12.clone.1 | loop fusion | flops 28311552 | bytes 8404992 | tf_op jit(solution)/shard_map/convert.7
  178.9 4.4 %subtract_convert_fusion.7 = (bf16[6,2,96,1,512]{4,2,3,1,0:T(8,128)(2,1)S(1)}, bf16[6,2,96,1,512]{4,2,3,1,0:T(8,128)(2,1)S(1)}, bf16[6,2,96,1,512]{4,2,3,1,0:T(8...) fusion(f32[96,512]{1,0:T(8,128)S(1)} %get-tuple-element.381, ...), kind=kLoop, calls=%fused_computation.12.clone.1 | loop fusion | flops 28311552 | bytes 8404992 | tf_op jit(solution)/shard_map/convert.7
  194.0 4.4 %subtract_convert_fusion.7 = (bf16[6,2,96,1,512]{4,2,3,1,0:T(8,128)(2,1)S(1)}, bf16[6,2,96,1,512]{4,2,3,1,0:T(8,128)(2,1)S(1)}, bf16[6,2,96,1,512]{4,2,3,1,0:T(8...) fusion(f32[96,512]{1,0:T(8,128)S(1)} %get-tuple-element.381, ...), kind=kLoop, calls=%fused_computation.12.clone.1 | loop fusion | flops 28311552 | bytes 8404992 | tf_op jit(solution)/shard_map/convert.7
  209.0 4.4 %subtract_convert_fusion.7 = (bf16[6,2,96,1,512]{4,2,3,1,0:T(8,128)(2,1)S(1)}, bf16[6,2,96,1,512]{4,2,3,1,0:T(8,128)(2,1)S(1)}, bf16[6,2,96,1,512]{4,2,3,1,0:T(8...) fusion(f32[96,512]{1,0:T(8,128)S(1)} %get-tuple-element.381, ...), kind=kLoop, calls=%fused_computation.12.clone.1 | loop fusion | flops 28311552 | bytes 8404992 | tf_op jit(solution)/shard_map/convert.7
  214.5 2.0 fusion.24
  224.0 4.4 %subtract_convert_fusion.7 = (bf16[6,2,96,1,512]{4,2,3,1,0:T(8,128)(2,1)S(1)}, bf16[6,2,96,1,512]{4,2,3,1,0:T(8,128)(2,1)S(1)}, bf16[6,2,96,1,512]{4,2,3,1,0:T(8...) fusion(f32[96,512]{1,0:T(8,128)S(1)} %get-tuple-element.381, ...), kind=kLoop, calls=%fused_computation.12.clone.1 | loop fusion | flops 28311552 | bytes 8404992 | tf_op jit(solution)/shard_map/convert.7
  239.0 4.4 %subtract_convert_fusion.7 = (bf16[6,2,96,1,512]{4,2,3,1,0:T(8,128)(2,1)S(1)}, bf16[6,2,96,1,512]{4,2,3,1,0:T(8,128)(2,1)S(1)}, bf16[6,2,96,1,512]{4,2,3,1,0:T(8...) fusion(f32[96,512]{1,0:T(8,128)S(1)} %get-tuple-element.381, ...), kind=kLoop, calls=%fused_computation.12.clone.1 | loop fusion | flops 28311552 | bytes 8404992 | tf_op jit(solution)/shard_map/convert.7
  254.0 4.4 %subtract_convert_fusion.7 = (bf16[6,2,96,1,512]{4,2,3,1,0:T(8,128)(2,1)S(1)}, bf16[6,2,96,1,512]{4,2,3,1,0:T(8,128)(2,1)S(1)}, bf16[6,2,96,1,512]{4,2,3,1,0:T(8...) fusion(f32[96,512]{1,0:T(8,128)S(1)} %get-tuple-element.381, ...), kind=kLoop, calls=%fused_computation.12.clone.1 | loop fusion | flops 28311552 | bytes 8404992 | tf_op jit(solution)/shard_map/convert.7
  259.5 2.0 fusion.24
  269.1 4.4 %subtract_convert_fusion.7 = (bf16[6,2,96,1,512]{4,2,3,1,0:T(8,128)(2,1)S(1)}, bf16[6,2,96,1,512]{4,2,3,1,0:T(8,128)(2,1)S(1)}, bf16[6,2,96,1,512]{4,2,3,1,0:T(8...) fusion(f32[96,512]{1,0:T(8,128)S(1)} %get-tuple-element.381, ...), kind=kLoop, calls=%fused_computation.12.clone.1 | loop fusion | flops 28311552 | bytes 8404992 | tf_op jit(solution)/shard_map/convert.7
  284.1 4.4 %subtract_convert_fusion.7 = (bf16[6,2,96,1,512]{4,2,3,1,0:T(8,128)(2,1)S(1)}, bf16[6,2,96,1,512]{4,2,3,1,0:T(8,128)(2,1)S(1)}, bf16[6,2,96,1,512]{4,2,3,1,0:T(8...) fusion(f32[96,512]{1,0:T(8,128)S(1)} %get-tuple-element.381, ...), kind=kLoop, calls=%fused_computation.12.clone.1 | loop fusion | flops 28311552 | bytes 8404992 | tf_op jit(solution)/shard_map/convert.7
  299.1 4.4 %subtract_convert_fusion.7 = (bf16[6,2,96,1,512]{4,2,3,1,0:T(8,128)(2,1)S(1)}, bf16[6,2,96,1,512]{4,2,3,1,0:T(8,128)(2,1)S(1)}, bf16[6,2,96,1,512]{4,2,3,1,0:T(8...) fusion(f32[96,512]{1,0:T(8,128)S(1)} %get-tuple-element.381, ...), kind=kLoop, calls=%fused_computation.12.clone.1 | loop fusion | flops 28311552 | bytes 8404992 | tf_op jit(solution)/shard_map/convert.7
  304.6 2.0 fusion.24
  311.4 95.9 %all-gather.6.cloned.1.call-done = f32[48,2,18432]{2,1,0:T(2,128)} async-done(((f32[6,2,18432]{2,1,0:T(2,128)}), f32[48,2,18432]{2,1,0:T(2,128)}) %all-gather.6.cloned.1.call-update) | async-done | bytes 7077904 | tf_op jit(solution)/shard_map/all_gather | solution.py:98
  407.3 6.4 %copy.46 = f32[8,6,2,18432]{3,2,1,0:T(2,128)} copy(f32[8,6,2,18432]{3,2,1,0:T(2,128)} %bitcast.88) | data formatting | bytes 14155776
  (436 shorter events, 161.6 us)
Async XLA Ops:
  6.5 63.2 %all-gather.4.cloned.1.call-start = ((), (), s32[]{:S(2)}) async-start(), calls=%async_computation | async-start | bytes 10027008 | tf_op jit(solution)/shard_map/all_gather | solution.py:75
  7.3 400.1 %all-gather.6.cloned.1.call-start = ((), (), s32[]{:S(2)}) async-start(), calls=%async_computation.1 | async-start | bytes 7962624 | tf_op jit(solution)/shard_map/all_gather | solution.py:98
Sparse Core Ops, SparseCore 0:
  9.0 60.6 all-gather.3
  311.5 95.7 all-gather.5
where the time goes:
time: 422 us; the launch traced here: 421 us
  waiting for transfers between devices  158 us (37%)
  other arithmetic  109 us (26%)
  local copies, waits for them, and re-layouts  105 us (25%)
  matrix products  32.4 us (8%)
  between operations  13.4 us (3%)
    all_gather x1, waiting for transfers between devices, body(): gathered = lax.all_gather(finished[None], 'tm', axis=0, tiled=True)  95.9 us
    another operation x16, other arithmetic  71.1 us
    all_gather x1, waiting for transfers between devices, body(): lax.all_gather(local.reshape(6 * nvec, sites), 'space', axis=1, tiled=True)  60.9 us
    dot_general x16, matrix products, advance(): jnp.einsum('imjqcg,qcrkg->imjrk', crossed, mixing(vec_block), preferred_e...  32.4 us
    reshape x16, local copies, waits for them, and re-layouts, advance(): return acc + part.reshape(rows, moments, width)  25.2 us
    gather x32, local copies, waits for them, and re-layouts, advance(): jnp.take(offsets, brick_ids, axis=0)  18.3 us
    dynamic_slice x16, local copies, waits for them, and re-layouts, advance(): lax.dynamic_slice_in_dim(vec_piece, index * block, block, 1)  17.7 us
    slice x16, local copies, waits for them, and re-layouts, cross_rows(): real_v = vecs[0].astype(jnp.float32)  17.6 us
  transfers between devices with their start and end apart: 2, of which 2 were waited for; matrix products, arithmetic and copies ran while one was open for 0% of the time, Pallas kernels for 0%

commit v1 on v0

--- a/solution.py
+++ b/solution.py
@@ -72,7 +72,12 @@
     moments = momenta.shape[0]
     mine = lax.axis_index("space") * rows
     empty = jnp.zeros((rows, moments, width), jnp.float32)
-    vec_piece = lax.all_gather(local.reshape(6 * nvec, sites), "space", axis=1, tiled=True)
+    vec_piece = jnp.concatenate(
+        lax.all_to_all(
+            jnp.stack([local.reshape(6 * nvec, sites)] * lax.axis_size("space")), "space", 0, 0
+        ),
+        axis=1,
+    )
     length = vec_piece.shape[1]
     block = math.gcd(length, sites)
 

time: 422 us -> 526 us (1.25)
  waiting for transfers between devices: 158 us -> 242 us
  local copies, waits for them, and re-layouts: 105 us -> 118 us
  starting transfers between devices: 0.04 us -> 7.08 us
    all_to_all x0 -> x1, waiting for transfers between devices: none -> 139 us  [body(): lax.all_to_all(jnp.stack([local.reshape(6 * nvec, sites)] * lax.axis_size...]
    all_gather x1 -> x0, waiting for transfers between devices: 60.9 us -> none  [body(): lax.all_gather(local.reshape(6 * nvec, sites), 'space', axis=1, tiled=True)]
    reshape x0 -> x1, local copies, waits for them, and re-layouts: none -> 8.74 us  [body(): jnp.concatenate(lax.all_to_all(jnp.stack([local.reshape(6 * nvec, sites)]...]
    all_to_all x0 -> x1, starting transfers between devices: none -> 7.05 us  [body(): lax.all_to_all(jnp.stack([local.reshape(6 * nvec, sites)] * lax.axis_size...]
    all_gather x1, waiting for transfers between devices: 95.9 us -> 103 us  [body(): gathered = lax.all_gather(finished[None], 'tm', axis=0, tiled=True)]
    another operation x0 -> x1, local copies, waits for them, and re-layouts: none -> 5.63 us  [body(): jnp.stack([local.reshape(6 * nvec, sites)] * lax.axis_size('space'))]
where the time goes in v1:
time: 526 us; the launch traced here: 525 us
  waiting for transfers between devices  242 us (46%)
  local copies, waits for them, and re-layouts  118 us (22%)
  other arithmetic  109 us (21%)
  matrix products  32.4 us (6%)
  between operations  13.4 us (3%)
  starting transfers between devices  7.08 us (1%)
    all_to_all x1, waiting for transfers between devices, body(): lax.all_to_all(jnp.stack([local.reshape(6 * nvec, sites)] * lax.axis_size...  139 us
    all_gather x1, waiting for transfers between devices, body(): gathered = lax.all_gather(finished[None], 'tm', axis=0, tiled=True)  103 us
    another operation x16, other arithmetic  71.1 us
    dot_general x16, matrix products, advance(): jnp.einsum('imjqcg,qcrkg->imjrk', crossed, mixing(vec_block), preferred_e...  32.4 us
    reshape x16, local copies, waits for them, and re-layouts, advance(): return acc + part.reshape(rows, moments, width)  25.2 us
    gather x32, local copies, waits for them, and re-layouts, advance(): jnp.take(offsets, brick_ids, axis=0)  18.3 us
    dynamic_slice x16, local copies, waits for them, and re-layouts, advance(): lax.dynamic_slice_in_dim(vec_piece, index * block, block, 1)  17.7 us
    slice x16, local copies, waits for them, and re-layouts, cross_rows(): real_v = vecs[0].astype(jnp.float32)  17.6 us
  transfers between devices with their start and end apart: 2, of which 2 were waited for; matrix products, arithmetic and copies ran while one was open for 0% of the time, Pallas kernels for 0%

profile of v1, /device:TPU:1, one launch (start us, length us, event | category | flops | bytes accessed | tf_op | source)
XLA Modules:
  0.0 524.8 jit_solution(6195186597421942202)
XLA Ops:
  6.5 5.6 %stack.165 = bf16[16,576,512]{2,1,0:T(8,128)(2,1)} broadcast(bf16[576,512]{1,0:T(8,128)(2,1)} %bitcast.93), dimensions={1,2} | broadcast | bytes 10027008 | tf_op jit(solution)/shard_map/stack | solution.py:77
  12.2 7.0 %all-to-all-start = ((bf16[16,576,512]{2,1,0:T(8,128)(2,1)}), bf16[16,576,512]{2,1,0:T(8,128)(2,1)}, u32[]{:S(2)}, u32[]{:S(2)}) async-start(bf16[16,576,512]{2,1,0:T(8,128)(2,1)} %stack.165), calls=%async_computation | async-start | bytes 18874368 | tf_op jit(solution)/shard_map/all_to_all | solution.py:76
  19.5 139.1 %all-to-all-done = bf16[16,576,512]{2,1,0:T(8,128)(2,1)} async-done(((bf16[16,576,512]{2,1,0:T(8,128)(2,1)}), bf16[16,576,512]{2,1,0:T(8,128)(2,1)}, u32[]{:S(2)}, u32[]{:S(2)}) %all-to-all-start) | async-done | bytes 9437216 | tf_op jit(solution)/shard_map/all_to_all | solution.py:76
  158.6 8.7 %copy.44 = bf16[16,72,8,512]{3,2,0,1:T(8,128)(2,1)} copy(bf16[16,72,8,512]{3,2,1,0:T(8,128)(2,1)} %bitcast.37) | data formatting | bytes 18874368 | tf_op jit(solution)/shard_map/reshape | solution.py:75
  167.3 240.3 %while.17 = (s32[]{:T(128)}, f32[6,2,18432]{2,1,0:T(2,128)S(1)}, s32[2,3]{0,1:T(4,128)S(1)}, s32[16,3]{1,0:T(8,128)S(1)}, bf16[576,8192]{1,0:T(8,128)(2,1)}, /*i...) while((s32[]{:T(128)}, f32[6,2,18432]{2,1,0:T(2,128)S(1)}, ...), condition=%wide.region_2.3_spmd.clone, body=%wide.region_0.2_spmd.clone.sunk | while | flops 1412249600 | bytes 46142696 | solution.py:101
  171.4 4.4 subtract_convert_fusion.7
  186.4 4.4 subtract_convert_fusion.7
  191.9 2.0 fusion.24
  201.4 4.4 subtract_convert_fusion.7
  216.5 4.4 subtract_convert_fusion.7
  231.5 4.4 subtract_convert_fusion.7
  246.5 4.4 subtract_convert_fusion.7
  261.5 4.4 subtract_convert_fusion.7
  276.5 4.4 subtract_convert_fusion.7
  291.6 4.4 subtract_convert_fusion.7
  306.6 4.4 subtract_convert_fusion.7
  321.6 4.4 subtract_convert_fusion.7
  336.6 4.4 subtract_convert_fusion.7
  351.6 4.4 subtract_convert_fusion.7
  366.7 4.4 subtract_convert_fusion.7
  381.7 4.4 subtract_convert_fusion.7
  396.7 4.4 subtract_convert_fusion.7
  409.0 102.5 %all-gather.3.cloned.1.call-done = f32[48,2,18432]{2,1,0:T(2,128)} async-done(((f32[6,2,18432]{2,1,0:T(2,128)}), f32[48,2,18432]{2,1,0:T(2,128)}) %all-gather.3.cloned.1.call-update) | async-done | bytes 7077904 | tf_op jit(solution)/shard_map/all_gather | solution.py:103
  511.5 6.4 %copy.56 = f32[8,6,2,18432]{3,2,1,0:T(2,128)} copy(f32[8,6,2,18432]{3,2,1,0:T(2,128)} %bitcast.92) | data formatting | bytes 14155776
  (441 shorter events, 165.6 us)
Async XLA Ops:
  12.2 7.1 %copy-start = (s32[16,3]{0,1:T(4,128)S(1)}, s32[16,3]{0,1:T(4,128)}, u32[]{:S(2)}) copy-start(s32[16,3]{0,1:T(4,128)} %param.7) | copy-start | bytes 580
  12.2 7.2 %copy-start.1 = (s32[2,3]{1,0:T(2,128)S(1)}, s32[2,3]{1,0:T(2,128)}, u32[]{:S(2)}) copy-start(s32[2,3]{1,0:T(2,128)} %param.6) | copy-start | bytes 76
  12.2 146.4 %all-to-all-start = ((bf16[16,576,512]{2,1,0:T(8,128)(2,1)}), bf16[16,576,512]{2,1,0:T(8,128)(2,1)}, u32[]{:S(2)}, u32[]{:S(2)}) async-start(bf16[16,576,512]{2,1,0:T(8,128)(2,1)} %stack.165), calls=%async_computation | async-start | bytes 18874368 | tf_op jit(solution)/shard_map/all_to_all | solution.py:76
  19.2 492.3 %all-gather.3.cloned.1.call-start = ((), (), s32[]{:S(2)}) async-start(), calls=%async_computation.1 | async-start | bytes 7962624 | tf_op jit(solution)/shard_map/all_gather | solution.py:103
Sparse Core Ops, SparseCore 0:
  409.1 102.3 all-gather.2
